TPU v7x, 32 devices: a whole 2x2x4 slice. The times are simulated.
32 devices in a mesh: group: 1, path: 32 (over z, y, x, core).
Axes of the slice: x: 2, y: 2, z: 4, core: 2. Of those that a mesh axis runs over, the one named last changes fastest.
Arguments:
- normals: float32 [8, 32, 8192], P(None, None, ('group', 'path')), may hold values from -6 to 6
- start_state: float32 [32, 8192], P(None, ('group', 'path')), may hold values from -0.12 to 0.12
- later_adjoint: float32 [32, 8192], P(None, ('group', 'path')), may hold values from -1.8 to 1.8
- vol: float32 [8], replicated, may hold values from 0.004 to 0.016
- factor_load: float32 [32, 960], replicated, may hold values from -2.1 to 2.1
- knots: float32 [960], replicated, may hold values from 0.01 to 0.05
- spline_jac: float32 [960, 960], replicated
- cashflows: bfloat16 [256, 960], P(('group', 'path')), may hold values from -0.1875 to 0.1875
- trade_set: int32 [256, 1], P(('group', 'path')), may hold values from 0 to 127
- trade_end: int32 [256], P(('group', 'path')), may hold values from 240 to 960
- set_cpty: int32 [128, 1], P('group'), may hold values from 0 to 63
- default_prob: float32 [8, 64], replicated, may hold values from 0.01 to 0.1
- base_value: float32 [8, 128], P(None, 'group'), may hold values from -3 to 3
Outputs:
- knot_grad: float32 [960], P('group')
- alloc: float32 [256], P(('group', 'path'))
- start_adjoint: float32 [32, 8192], P(None, ('group', 'path'))
All inputs are finite; a program needn't handle non-finite values.
Results may differ from a plain program's by a relative error of at most 0.0011.
Values may be sent and summed in bfloat16 or wider, within the bound.
No kernel may reach another device: no remote copies, remote signals or barrier semaphores. Data moves between devices by JAX's collectives and lax.ppermute only.
A program may use at most 64 MiB of HBM per device.

v0:
```python
import math
import jax
import jax.numpy as jnp
from jax import lax
from jax.sharding import PartitionSpec as P

MEAN_REV = 0.05
STEP_YEARS = 0.25
HORIZON_YEARS = 30.0
SHARPNESS = 4.0
LOSS_RATE = 0.6


def curve_terms(knots, spline_jac, date_count, knot_count):
    zero_rate = jnp.dot(spline_jac, knots, precision=lax.Precision.HIGHEST)
    knot_index = jnp.arange(knot_count, dtype=jnp.int32)
    date_index = jnp.arange(date_count, dtype=jnp.int32)
    is_alive = 120 * (knot_index[None, :] + 1) > knot_count * (date_index[:, None] + 1)
    maturity = HORIZON_YEARS * (knot_index + 1).astype(jnp.float32) / knot_count
    fixing = STEP_YEARS * (date_index + 1).astype(jnp.float32)
    horizon = jnp.where(is_alive, maturity[None, :] - fixing[:, None], jnp.float32(0.0))
    loading = (1.0 - jnp.exp(-MEAN_REV * horizon)) / MEAN_REV
    discount = jnp.where(is_alive, jnp.exp(-zero_rate[None, :] * horizon), jnp.float32(0.0))
    return (horizon, loading, discount)


def state_path(start_state, vol, normals):
    decay_factor = math.exp(-MEAN_REV * STEP_YEARS)
    state = start_state
    collected = []
    for index in range(normals.shape[0]):
        state = decay_factor * state + vol[index] * normals[index]
        collected.append(state)
    return jnp.stack(collected)


def per_device(
    normals,
    start_state,
    later_adjoint,
    vol,
    factor_load,
    knots,
    spline_jac,
    cashflows,
    trade_set,
    trade_end,
    set_cpty,
    default_prob,
    base_value,
):
    highest = lax.Precision.HIGHEST
    date_count = normals.shape[0]
    knot_count = knots.shape[0]
    set_count = base_value.shape[1]
    paths_all = normals.shape[2] * lax.axis_size("path")
    horizon, loading, discount = curve_terms(knots, spline_jac, date_count, knot_count)
    knot_index = jnp.arange(knot_count, dtype=jnp.int32)
    live_flows = jnp.where(
        knot_index[None, :] < trade_end[:, None], cashflows, jnp.zeros_like(cashflows)
    )
    set_ids = trade_set[:, 0]
    labels = jnp.arange(set_count, dtype=jnp.int32)
    all_flows, all_sets = (
        lax.all_gather(live_flows, "path", axis=0, tiled=True),
        lax.all_gather(set_ids, "path", axis=0, tiled=True),
    )
    member = (labels[:, None] == all_sets[None, :]).astype(jnp.bfloat16)
    net_flows = jnp.dot(member, all_flows, preferred_element_type=jnp.float32).astype(jnp.bfloat16)
    counter = (
        jnp.arange(default_prob.shape[1], dtype=jnp.int32)[:, None] == set_cpty[:, 0][None, :]
    ).astype(jnp.float32)
    weight = LOSS_RATE * jnp.dot(default_prob, counter, precision=highest)
    states = state_path(start_state, vol, normals)
    shift = jnp.einsum("fm,ifp->imp", factor_load, states, precision=highest)
    bond_term = jnp.exp(-loading[:, :, None] * shift)
    feat_exact = discount[:, :, None] * bond_term
    features = feat_exact.astype(jnp.bfloat16)
    values = jnp.einsum("nm,imp->inp", net_flows, features, preferred_element_type=jnp.float32)
    mean_value = lax.psum(jnp.sum(values, axis=2), "path") / paths_all
    shifted = values - mean_value[:, :, None] + base_value[:, :, None]
    slope = weight[:, :, None] * jax.nn.sigmoid(SHARPNESS * shifted)
    mean_slope = lax.psum(jnp.sum(slope, axis=2), "path") / paths_all
    set_adjoint = (slope - mean_slope[:, :, None]).astype(jnp.bfloat16)
    feat_adjoint = jnp.einsum(
        "nm,inp->imp", net_flows, set_adjoint, preferred_element_type=jnp.float32
    )
    state_local = -jnp.einsum(
        "fm,imp->ifp",
        factor_load,
        feat_adjoint * feat_exact * loading[:, :, None],
        precision=highest,
    )
    discount_grad = jnp.sum(feat_adjoint * bond_term, axis=2)
    rate_adjoint = -jnp.sum(discount_grad * discount * horizon, axis=0) / paths_all
    rate_total = lax.psum(rate_adjoint, "path")
    knot_grad = jnp.dot(spline_jac.T, rate_total, precision=highest)
    load_sums = (
        jnp.einsum("inp,imp->nm", set_adjoint, features, preferred_element_type=jnp.float32)
        / paths_all
    )
    set_rows = load_sums[all_sets]
    trade_part = jnp.sum(all_flows.astype(jnp.float32) * set_rows, axis=1)
    alloc = lax.psum_scatter(trade_part, "path", scatter_dimension=0, tiled=True)
    decay_factor = math.exp(-MEAN_REV * STEP_YEARS)
    carried = later_adjoint + state_local[date_count - 1]
    for index in reversed(range(date_count - 1)):
        carried = state_local[index] + decay_factor * carried
    start_adjoint = decay_factor * carried
    return (knot_grad, alloc, start_adjoint)


def solution(mesh):
    in_specs = (
        P(None, None, ("group", "path")),
        P(None, ("group", "path")),
        P(None, ("group", "path")),
        P(),
        P(),
        P(),
        P(),
        P(("group", "path"), None),
        P(("group", "path"), None),
        P(("group", "path")),
        P("group", None),
        P(),
        P(None, "group"),
    )
    out_specs = (P("group"), P(("group", "path")), P(None, ("group", "path")))
    return jax.shard_map(
        per_device, mesh=mesh, in_specs=in_specs, out_specs=out_specs, check_vma=False
    )
```

profile of v0, /device:TPU:0, one launch (start us, length us, event | category | flops | bytes accessed | tf_op | source)
XLA Modules:
  0.0 270.6 jit_solution(15762425865365894682)
XLA Ops:
  0.6 0.0 copy-start
  0.7 0.0 copy-start.16
  0.7 0.0 copy-start.18
  0.7 0.8 bitcast_dynamic-update-slice_fusion.8
  1.5 41.9 %all-reduce = s32[256]{0:T(256)S(1)} all-reduce(s32[256]{0:T(256)S(1)} %bitcast_dynamic-update-slice_fusion.8), channel_id=2, replica_groups=mesh['group'=1,'path'=32] {'path'}, use_global_device_ids=true, to_apply=%add | all-reduce | flops 256 | bytes 2048 | tf_op jit(solution)/shard_map/all_gather | solution.py:66
  43.4 0.6 pad_clamp_fusion
  44.0 0.8 fusion.18
  44.8 0.0 copy-start.5
  44.9 0.0 copy-start.7
  44.9 5.4 %fusion.50 = f32[1,960]{1,0:T(1,128)S(1)} fusion(f32[960,960]{1,0:T(8,128)} %param.19, f32[960,1]{0,1:T(1,128)} %bitcast.192), kind=kOutput, calls=%fused_computation.96 | convolution fusion | flops 11059200 | bytes 3694080 | tf_op jit(solution)/shard_map/dot_general | solution.py:15
  50.3 1.6 fusion.48
  52.0 0.8 fusion.42
  52.8 0.7 subtract_multiply_fusion
  53.5 1.5 bitcast_dynamic-update-slice_fusion.7
  54.9 2.0 bitcast_dynamic-update-slice_fusion.6
  57.0 1.5 bitcast_dynamic-update-slice_fusion.5
  58.4 2.0 bitcast_dynamic-update-slice_fusion.4
  60.5 1.5 bitcast_dynamic-update-slice_fusion.3
  61.9 2.1 bitcast_dynamic-update-slice_fusion.2
  64.1 1.4 bitcast_dynamic-update-slice_fusion.1
  65.4 2.1 bitcast_dynamic-update-slice_fusion
  67.5 41.7 %all_gather.7 = bf16[256,960]{1,0:T(8,128)(2,1)S(1)} all-gather(bf16[8,960]{1,0:T(8,128)(2,1)S(1)} %fusion.42), channel_id=1, replica_groups=mesh['group'=1,'path'=32] {'path'}, dimensions={0}, use_global_device_ids=true | all-gather | bytes 506880 | tf_op jit(solution)/shard_map/all_gather | solution.py:65
  109.2 0.3 fusion.17
  109.6 0.0 copy-done
  109.6 0.0 copy-start.13
  109.6 6.5 %fusion.23 = f32[8,256,960]{1,2,0:T(8,128)S(1)} fusion(f32[8,32,256]{2,1,0:T(8,128)S(1)} %bitcast_dynamic-update-slice_fusion, f32[32,960]{1,0:T(8,128)S(1)} %copy-done), kind=kOutput, calls=%fused_computation.28 | convolution fusion | flops 754974720 | bytes 8249344 | tf_op jit(solution)/shard_map/fm,ifp->imp/dot_general | solution.py:75
  116.1 0.0 copy-start.1
  116.1 3.1 %copy-done.1 = f32[8,256,960]{1,2,0:T(8,128)} copy-done((f32[8,256,960]{1,2,0:T(8,128)}, f32[8,256,960]{1,2,0:T(8,128)S(1)}, u32[]{:S(2)}) %copy-start.1) | copy-done | bytes 7864344
  119.1 5.4 %fusion.49 = (f32[8,128]{1,0:T(8,128)S(1)}, f32[8,128,256]{1,2,0:T(8,128)S(1)}) fusion(bf16[128,960,1]{0,1,2:T(8,128)(2,1)S(1)} %fusion.17, f32[8,256,960]{1,2,0:T(8,128)S(1)} %fusion.23, f32[8,960]{1,0:T(8,128)S(1)} %get-tuple-element.12, f32[8,960]{1,0:T(8,128)S(1)} %get-tuple-element.13), kind=kOutput, calls=%fused_computation.95 | convolution fusion | flops 509475840 | bytes 9224192 | tf_op jit(solution)/shard_map/nm,imp->inp/dot_general | solution.py:79
  124.5 0.0 copy-done.16
  124.6 0.0 copy-done.18
  124.6 0.0 copy-done.5
  124.6 0.0 copy-done.7
  124.6 0.0 copy-done.9
  124.6 37.0 %psum.21 = f32[8,128]{1,0:T(8,128)S(1)} all-reduce(f32[8,128]{1,0:T(8,128)S(1)} %get-tuple-element.22), channel_id=1, replica_groups=mesh['group'=1,'path'=32] {'path'}, use_global_device_ids=true, to_apply=%region_1.2 | all-reduce | flops 1024 | bytes 8192 | tf_op jit(solution)/shard_map/psum | solution.py:80
  161.6 0.0 copy-done.13
  161.6 0.3 fusion.47
  162.0 41.2 %psum.22 = f32[8,128]{1,0:T(8,128)S(1)} all-reduce(f32[8,128]{1,0:T(8,128)S(1)} %fusion.47), channel_id=1, replica_groups=mesh['group'=1,'path'=32] {'path'}, use_global_device_ids=true, to_apply=%region_3.4 | all-reduce | flops 1024 | bytes 8192 | tf_op jit(solution)/shard_map/psum | solution.py:83
  203.1 0.0 copy-done.14
  203.1 0.0 copy-done.11
  203.2 0.0 copy-start.15
  203.2 0.6 copy-done.15
  203.8 5.4 %fusion.10 = f32[128,960]{0,1:T(8,128)S(1)} fusion(f32[8,256,960]{1,2,0:T(8,128)} %copy-done.1, f32[8,960]{1,0:T(8,128)S(1)} %get-tuple-element.12, f32[8,960]{1,0:T(8,128)S(1)} %get-tuple-element.13, f32[8,128]{1,0:T(8,128)S(1)} %broadcast_multiply_fusion, f32[8,128,256]{1,2,0:T(8,128)S(1)} %get-tuple-element.23, f32[8,128]{1,0:T(8,128)S(1)} %copy-done.13, ...), kind=kOutput, calls=%fused_computation.16 | convolution fusion | flops 511696896 | bytes 9482240 | tf_op jit(solution)/shard_map/inp,imp->nm/dot_general | solution.py:99
  209.2 0.2 copy.21
  209.4 1.2 gather_fusion
  210.6 0.0 slice-start
  210.6 0.2 multiply_reduce_fusion
  210.8 0.0 copy-start.3
  210.8 0.0 copy-start.4
  210.8 6.4 %fusion = (f32[8,960]{1,0:T(8,128)S(1)}, f32[8,256,960]{1,2,0:T(8,128)S(1)}) fusion(f32[8,256,960]{1,2,0:T(8,128)} %copy-done.1, f32[8,960]{1,0:T(8,128)S(1)} %get-tuple-element.12, bf16[128,960,1]{0,1,2:T(8,128)(2,1)S(1)} %fusion.17, f32[8,128]{1,0:T(8,128)} %copy-done.15, f32[8,128]{1,0:T(8,128)} %param.25, f32[8,128,256]{1,2,0:T(8,128)S(1)} %get-tuple-element.23, ...), kind=kOutput, calls=%fused_computation.3 | convolution fusion | flops 511566336 | bytes 17100800 | tf_op jit(solution)/shard_map/nm,inp->imp/dot_general | solution.py:85
  217.3 0.0 copy-start.12
  217.3 0.0 copy-start.6
  217.3 0.0 copy-start.8
  217.3 0.0 copy-start.10
  217.3 0.0 copy-start.17
  217.4 0.0 copy-start.19
  217.4 7.6 %fusion.14 = f32[8,32,256]{2,1,0:T(8,128)S(1)} fusion(f32[8,256,960]{1,2,0:T(8,128)S(1)} %get-tuple-element.25, f32[8,256,960]{1,2,0:T(8,128)S(1)} %bitcast.190, f32[8,960]{1,0:T(8,128)S(1)} %copy-done.4, f32[8,960]{1,0:T(8,128)S(1)} %get-tuple-element.12, f32[8,960]{1,0:T(8,128)S(1)} %copy-done.3, f32[32,960]{1,0:T(8,128)S(1)} %copy-done), kind=kOutput, calls=%fused_computation.19 | convolution fusion | flops 762904576 | bytes 16205824 | tf_op jit(solution)/shard_map/fm,imp->ifp/dot_general | solution.py:88
  224.9 0.0 copy-done.12
  225.0 0.6 fusion.41
  225.6 0.0 copy-done.8
  225.6 0.1 multiply_reduce_fusion.1
  225.7 39.6 %all-reduce.2 = (f32[960]{0:T(1024)S(1)}, f32[256]{0:T(256)S(1)}) all-reduce(f32[960]{0:T(1024)S(1)} %negate_multiply_fusion, f32[256]{0:T(256)S(1)} %multiply_reduce_fusion), channel_id=1, replica_groups=mesh['group'=1,'path'=32] {'path'}, use_global_device_ids=true, to_apply=%region_6.7 | all-reduce | flops 1216 | bytes 9728 | tf_op jit(solution)/shard_map/psum | solution.py:96
  265.3 4.7 %fusion.5 = f32[1,960]{1,0:T(1,128)} fusion(f32[960,1]{0,1:T(1,128)S(1)} %bitcast.194, f32[960,960]{1,0:T(8,128)} %param.19), kind=kOutput, calls=%fused_computation.9 | convolution fusion | flops 11059200 | bytes 3694080 | tf_op jit(solution)/shard_map/dot_general | solution.py:97
  270.0 0.6 dynamic-slice
  (25 shorter events, 0.1 us)
Async XLA Ops:
  0.6 108.9 %copy-start = (f32[32,960]{1,0:T(8,128)S(1)}, f32[32,960]{1,0:T(8,128)}, u32[]{:S(2)}) copy-start(f32[32,960]{1,0:T(8,128)} %param.17) | copy-start | bytes 368644
  0.7 123.9 %copy-start.16 = (s32[8]{0:T(128)}, s32[8]{0:T(128)S(1)}, u32[]{:S(2)}) copy-start(s32[8]{0:T(128)S(1)} %fusion.46) | copy-start | bytes 100
  0.7 123.9 %copy-start.18 = (f32[8]{0:T(128)}, f32[8]{0:T(128)S(1)}, u32[]{:S(2)}) copy-start(f32[8]{0:T(128)S(1)} %convert_multiply_fusion.1) | copy-start | bytes 100
  44.8 158.3 %copy-start.14 = (f32[8,128]{1,0:T(8,128)}, f32[8,128]{1,0:T(8,128)S(1)}, u32[]{:S(2)}) copy-start(f32[8,128]{1,0:T(8,128)S(1)} %fusion.18) | copy-start | bytes 12292
  44.8 79.7 %copy-start.5 = (s32[960]{0:T(1024)}, s32[960]{0:T(1024)S(1)}, u32[]{:S(2)}) copy-start(s32[960]{0:T(1024)S(1)} %fusion.44) | copy-start | bytes 11524
  44.9 79.7 %copy-start.7 = (f32[960]{0:T(1024)}, f32[960]{0:T(1024)S(1)}, u32[]{:S(2)}) copy-start(f32[960]{0:T(1024)S(1)} %convert_multiply_fusion) | copy-start | bytes 11524
  50.3 74.3 %copy-start.9 = (f32[960]{0:T(1024)}, f32[960]{0:T(1024)S(1)}, u32[]{:S(2)}) copy-start(f32[960]{0:T(1024)S(1)} %neg.24) | copy-start | bytes 11524
  53.5 149.7 %copy-start.2 = (f32[8,960]{1,0:T(8,128)}, f32[8,960]{1,0:T(8,128)S(1)}, u32[]{:S(2)}) copy-start(f32[8,960]{1,0:T(8,128)S(1)} %get-tuple-element.13) | copy-start | bytes 92164
  109.6 52.1 %copy-start.13 = (f32[8,128]{1,0:T(8,128)S(1)}, f32[8,128]{1,0:T(8,128)}, u32[]{:S(2)}) copy-start(f32[8,128]{1,0:T(8,128)} %param.25) | copy-start | bytes 12292
  116.1 3.1 %copy-start.1 = (f32[8,256,960]{1,2,0:T(8,128)}, f32[8,256,960]{1,2,0:T(8,128)S(1)}, u32[]{:S(2)}) copy-start(f32[8,256,960]{1,2,0:T(8,128)S(1)} %fusion.23) | copy-start | bytes 23592964
  161.6 41.5 %copy-start.11 = (f32[8,128]{1,0:T(8,128)}, f32[8,128]{1,0:T(8,128)S(1)}, u32[]{:S(2)}) copy-start(f32[8,128]{1,0:T(8,128)S(1)} %broadcast_multiply_fusion.1) | copy-start | bytes 12292
  203.2 0.6 copy-start.15
  210.6 6.7 %slice-start = ((s8[7864320]{0:T(1024)(128)(4,1)}), s8[4194304]{0:T(1024)(128)(4,1)S(1)}, s32[]{:S(2)}) async-start(s8[7864320]{0:T(1024)(128)(4,1)} %bitcast.189), calls=%async_computation | async-start | bytes 8388608
  210.8 6.5 %slice-start.1 = ((s8[7864320]{0:T(1024)(128)(4,1)}), s8[3670016]{0:T(1024)(128)(4,1)S(1)}, s32[]{:S(2)}) async-start(s8[7864320]{0:T(1024)(128)(4,1)} %bitcast.189), calls=%async_computation.1 | async-start | bytes 7340032
  210.8 6.5 %copy-start.3 = (f32[8,960]{1,0:T(8,128)S(1)}, f32[8,960]{1,0:T(8,128)}, u32[]{:S(2)}) copy-start(f32[8,960]{1,0:T(8,128)} %copy-done.2) | copy-start | bytes 92164
  210.8 6.5 %copy-start.4 = (f32[8,960]{1,0:T(8,128)S(1)}, f32[8,960]{1,0:T(8,128)}, u32[]{:S(2)}) copy-start(f32[8,960]{1,0:T(8,128)} %get-tuple-element.11) | copy-start | bytes 92164
  217.3 7.6 %copy-start.12 = (f32[32,256]{1,0:T(8,128)S(1)}, f32[32,256]{1,0:T(8,128)}, u32[]{:S(2)}) copy-start(f32[32,256]{1,0:T(8,128)} %param.15) | copy-start | bytes 98308
  217.3 8.3 %copy-start.6 = (s32[960]{0:T(1024)S(1)}, s32[960]{0:T(1024)}, u32[]{:S(2)}) copy-start(s32[960]{0:T(1024)} %copy-done.5) | copy-start | bytes 11524
  217.3 8.3 %copy-start.8 = (f32[960]{0:T(1024)S(1)}, f32[960]{0:T(1024)}, u32[]{:S(2)}) copy-start(f32[960]{0:T(1024)} %copy-done.7) | copy-start | bytes 11524
  217.3 8.3 %copy-start.10 = (f32[960]{0:T(1024)S(1)}, f32[960]{0:T(1024)}, u32[]{:S(2)}) copy-start(f32[960]{0:T(1024)} %copy-done.9) | copy-start | bytes 11524
  217.3 8.3 %copy-start.17 = (s32[8]{0:T(128)S(1)}, s32[8]{0:T(128)}, u32[]{:S(2)}) copy-start(s32[8]{0:T(128)} %copy-done.16) | copy-start | bytes 100
  217.4 8.3 %copy-start.19 = (f32[8]{0:T(128)S(1)}, f32[8]{0:T(128)}, u32[]{:S(2)}) copy-start(f32[8]{0:T(128)} %copy-done.18) | copy-start | bytes 100
where the time goes:
time: 272 us; the launch traced here: 271 us
  blocking collectives  201 us (74%)
  matrix products  42.6 us (16%)
  other arithmetic  17.4 us (6%)
  local copies, waits for them, and re-layouts  8.13 us (3%)
    all_gather x1, blocking collectives, per_device(): lax.all_gather(set_ids, 'path', axis=0, tiled=True)  41.9 us
    all_gather x1, blocking collectives, per_device(): lax.all_gather(live_flows, 'path', axis=0, tiled=True)  41.7 us
    psum x1, blocking collectives, per_device(): mean_slope = lax.psum(jnp.sum(slope, axis=2), 'path') / paths_all  41.2 us
    psum x1, blocking collectives, per_device(): rate_total = lax.psum(rate_adjoint, 'path')  39.6 us
    psum x1, blocking collectives, per_device(): mean_value = lax.psum(jnp.sum(values, axis=2), 'path') / paths_all  37 us
    unnamed x8, other arithmetic  12 us
    dot_general x1, matrix products, per_device(): jnp.einsum('fm,imp->ifp', factor_load, feat_adjoint * feat_exact * loadin...  7.57 us
    dot_general x1, matrix products, per_device(): shift = jnp.einsum('fm,ifp->imp', factor_load, states, precision=highest)  6.46 us

commit v1 on v0

--- a/solution.py
+++ b/solution.py
@@ -93,7 +93,7 @@
     )
     discount_grad = jnp.sum(feat_adjoint * bond_term, axis=2)
     rate_adjoint = -jnp.sum(discount_grad * discount * horizon, axis=0) / paths_all
-    rate_total = lax.psum(rate_adjoint, "path")
+    rate_total = jnp.sum(lax.all_gather(rate_adjoint, "path"), axis=0)
     knot_grad = jnp.dot(spline_jac.T, rate_total, precision=highest)
     load_sums = (
         jnp.einsum("inp,imp->nm", set_adjoint, features, preferred_element_type=jnp.float32)

time: 272 us -> 353 us (1.30)
  waiting for transfers between devices: 0 us -> 64.9 us
  between operations: 1.04 us -> 14.3 us
    unnamed x0 -> x2, waiting for transfers between devices: none -> 64.9 us
    unnamed x0 -> x1, blocking collectives: none -> 39.6 us
    psum x1 -> x0, blocking collectives: 39.6 us -> none  [per_device(): rate_total = lax.psum(rate_adjoint, 'path')]
  transfers between devices with their start and end apart: 0 -> 1, of which waited for: 0 -> 1; matrix products, arithmetic and copies ran while one was open for 0% -> 5% of each run, Pallas kernels for 0% -> 0%
where the time goes in v1:
time: 353 us; the launch traced here: 352 us
  blocking collectives  201 us (57%)
  waiting for transfers between devices  64.9 us (18%)
  matrix products  46 us (13%)
  other arithmetic  16.1 us (5%)
  between operations  14.3 us (4%)
  local copies, waits for them, and re-layouts  8.9 us (3%)
    unnamed x2, waiting for transfers between devices  64.9 us
    all_gather x1, blocking collectives, per_device(): lax.all_gather(set_ids, 'path', axis=0, tiled=True)  42 us
    all_gather x1, blocking collectives, per_device(): lax.all_gather(live_flows, 'path', axis=0, tiled=True)  41.7 us
    psum x1, blocking collectives, per_device(): mean_slope = lax.psum(jnp.sum(slope, axis=2), 'path') / paths_all  41.2 us
    unnamed x1, blocking collectives  39.6 us
    psum x1, blocking collectives, per_device(): mean_value = lax.psum(jnp.sum(values, axis=2), 'path') / paths_all  37.1 us
    unnamed x8, other arithmetic  11.8 us
    dot_general x1, matrix products, per_device(): jnp.einsum('fm,imp->ifp', factor_load, feat_adjoint * feat_exact * loadin...  11.1 us
  transfers between devices with their start and end apart: 1, of which 1 were waited for; matrix products, arithmetic and copies ran while one was open for 5% of the time, Pallas kernels for 0%

profile of v1, /device:TPU:0, one launch (start us, length us, event | category | flops | bytes accessed | tf_op | source)
XLA Modules:
  0.0 351.6 jit_solution(9350441267751391414)
XLA Ops:
  7.2 0.0 copy-start
  7.2 0.0 all-reduce.5.cloned.1.call-start
  7.3 0.8 bitcast_dynamic-update-slice_fusion.8
  8.0 42.0 %all-reduce = s32[256]{0:T(256)S(1)} all-reduce(s32[256]{0:T(256)S(1)} %bitcast_dynamic-update-slice_fusion.8), channel_id=2, replica_groups=mesh['group'=1,'path'=32] {'path'}, use_global_device_ids=true, to_apply=%add | all-reduce | flops 256 | bytes 2048 | tf_op jit(solution)/shard_map/all_gather | solution.py:66
  50.0 5.4 %fusion.50 = f32[1,960]{1,0:T(1,128)S(1)} fusion(f32[960,960]{1,0:T(8,128)} %param.19, f32[960,1]{0,1:T(1,128)} %bitcast.191), kind=kOutput, calls=%fused_computation.96 | convolution fusion | flops 11059200 | bytes 3694080 | tf_op jit(solution)/shard_map/dot_general | solution.py:15
  55.4 1.6 fusion.48
  57.1 0.8 fusion.42
  57.9 41.7 %all_gather.11 = bf16[256,960]{1,0:T(8,128)(2,1)S(1)} all-gather(bf16[8,960]{1,0:T(8,128)(2,1)S(1)} %fusion.42), channel_id=1, replica_groups=mesh['group'=1,'path'=32] {'path'}, dimensions={0}, use_global_device_ids=true | all-gather | bytes 506880 | tf_op jit(solution)/shard_map/all_gather | solution.py:65
  99.6 1.4 bitcast_dynamic-update-slice_fusion.7
  101.0 2.1 bitcast_dynamic-update-slice_fusion.6
  103.0 1.3 bitcast_dynamic-update-slice_fusion.5
  104.4 2.0 bitcast_dynamic-update-slice_fusion.4
  106.4 1.4 bitcast_dynamic-update-slice_fusion.3
  107.8 2.1 bitcast_dynamic-update-slice_fusion.2
  109.9 1.4 bitcast_dynamic-update-slice_fusion.1
  111.3 2.0 bitcast_dynamic-update-slice_fusion
  113.3 0.3 fusion.17
  113.7 0.0 copy-done
  113.7 0.0 copy-start.5
  113.7 0.0 copy-start.6
  113.7 0.0 copy-start.4
  113.7 6.5 %fusion.23 = f32[8,256,960]{1,2,0:T(8,128)S(1)} fusion(f32[8,32,256]{2,1,0:T(8,128)S(1)} %bitcast_dynamic-update-slice_fusion, f32[32,960]{1,0:T(8,128)S(1)} %copy-done), kind=kOutput, calls=%fused_computation.28 | convolution fusion | flops 754974720 | bytes 8249344 | tf_op jit(solution)/shard_map/fm,ifp->imp/dot_general | solution.py:75
  120.2 0.0 copy-start.1
  120.2 0.1 subtract_multiply_fusion
  120.3 3.0 copy-done.1
  123.3 5.4 %fusion.49 = (f32[8,128]{1,0:T(8,128)S(1)}, f32[8,128,256]{1,2,0:T(8,128)S(1)}) fusion(bf16[128,960,1]{0,1,2:T(8,128)(2,1)S(1)} %fusion.17, f32[8,256,960]{1,2,0:T(8,128)S(1)} %fusion.23, f32[8,960]{1,0:T(8,128)S(1)} %get-tuple-element.10, f32[8,960]{1,0:T(8,128)S(1)} %get-tuple-element.11), kind=kOutput, calls=%fused_computation.95 | convolution fusion | flops 509475840 | bytes 9224192 | tf_op jit(solution)/shard_map/nm,imp->inp/dot_general | solution.py:79
  128.7 37.1 %psum.14 = f32[8,128]{1,0:T(8,128)S(1)} all-reduce(f32[8,128]{1,0:T(8,128)S(1)} %get-tuple-element.20), channel_id=1, replica_groups=mesh['group'=1,'path'=32] {'path'}, use_global_device_ids=true, to_apply=%region_1.2 | all-reduce | flops 1024 | bytes 8192 | tf_op jit(solution)/shard_map/psum | solution.py:80
  165.7 0.0 copy-done.5
  165.7 0.0 copy-done.6
  165.8 0.1 fusion.18
  165.9 0.0 copy-done.4
  165.9 0.3 fusion.47
  166.2 41.2 %psum.15 = f32[8,128]{1,0:T(8,128)S(1)} all-reduce(f32[8,128]{1,0:T(8,128)S(1)} %fusion.47), channel_id=1, replica_groups=mesh['group'=1,'path'=32] {'path'}, use_global_device_ids=true, to_apply=%region_3.4 | all-reduce | flops 1024 | bytes 8192 | tf_op jit(solution)/shard_map/psum | solution.py:83
  207.4 7.0 %fusion = (f32[8,960]{1,0:T(8,128)S(1)}, f32[8,256,960]{1,2,0:T(8,128)}) fusion(f32[8,256,960]{1,2,0:T(8,128)} %copy-done.1, f32[8,960]{1,0:T(8,128)S(1)} %get-tuple-element.10, bf16[128,960,1]{0,1,2:T(8,128)(2,1)S(1)} %fusion.17, f32[8,128]{1,0:T(8,128)S(1)} %broadcast_multiply_fusion, f32[8,128]{1,0:T(8,128)S(1)} %copy-done.4, ...), kind=kOutput, calls=%fused_computation.3 | convolution fusion | flops 511566336 | bytes 17100800 | tf_op jit(solution)/shard_map/nm,inp->imp/dot_general | solution.py:85
  214.4 0.1 multiply_reduce_fusion.1
  214.6 0.1 multiply_dynamic-update-slice_fusion
  214.7 0.0 copy-start.2
  214.7 0.6 copy-done.2
  215.3 0.0 all-reduce.5.cloned.1.call-update
  215.4 5.4 %fusion.10 = f32[128,960]{0,1:T(8,128)S(1)} fusion(f32[8,256,960]{1,2,0:T(8,128)} %copy-done.1, f32[8,960]{1,0:T(8,128)S(1)} %get-tuple-element.10, f32[8,960]{1,0:T(8,128)S(1)} %get-tuple-element.11, f32[8,128]{1,0:T(8,128)S(1)} %broadcast_multiply_fusion, f32[8,128,256]{1,2,0:T(8,128)S(1)} %get-tuple-element.21, f32[8,128]{1,0:T(8,128)S(1)} %copy-done.4, ...), kind=kOutput, calls=%fused_computation.16 | convolution fusion | flops 511696896 | bytes 9482240 | tf_op jit(solution)/shard_map/inp,imp->nm/dot_general | solution.py:99
  220.8 0.2 copy.24
  221.0 1.1 gather_fusion
  222.1 0.0 copy-start.3
  222.1 11.1 %fusion.14 = f32[8,32,256]{2,1,0:T(8,128)S(1)} fusion(f32[8,256,960]{1,2,0:T(8,128)} %get-tuple-element.23, f32[8,256,960]{1,2,0:T(8,128)} %copy-done.1, f32[8,960]{1,0:T(8,128)S(1)} %get-tuple-element.9, f32[8,960]{1,0:T(8,128)S(1)} %get-tuple-element.10, f32[8,960]{1,0:T(8,128)S(1)} %get-tuple-element.11, f32[32,960]{1,0:T(8,128)S(1)} %copy-done), kind=kOutput, calls=%fused_computation.19 | convolution fusion | flops 762904576 | bytes 16205824 | tf_op jit(solution)/shard_map/fm,imp->ifp/dot_general | solution.py:88
  233.2 0.0 copy-done.3
  233.2 0.6 fusion.41
  233.8 0.2 multiply_reduce_fusion
  234.0 39.6 %all-reduce.2 = f32[256]{0:T(256)S(1)} all-reduce(f32[256]{0:T(256)S(1)} %multiply_reduce_fusion), channel_id=4, replica_groups=mesh['group'=1,'path'=32] {'path'}, use_global_device_ids=true, to_apply=%region_8.9.clone | all-reduce | flops 256 | bytes 2048
  273.6 0.6 dynamic-slice
  274.2 64.8 %all-reduce.5.cloned.1.call-done = f32[30720]{0:T(1024)} async-done(((f32[30720]{0:T(1024)}), f32[30720]{0:T(1024)}) %all-reduce.5.cloned.1.call-update) | async-done | bytes 122896
  339.0 1.0 reshape.253
  340.0 4.7 %fusion.5 = f32[1,960]{1,0:T(1,128)} fusion(f32[960,1]{0,1:T(1,128)S(1)} %bitcast.189, f32[960,960]{1,0:T(8,128)} %param.19), kind=kOutput, calls=%fused_computation.9 | convolution fusion | flops 11059200 | bytes 3694080 | tf_op jit(solution)/shard_map/dot_general | solution.py:97
  (12 shorter events, 0.1 us)
Async XLA Ops:
  7.2 106.5 %copy-start = (f32[32,960]{1,0:T(8,128)S(1)}, f32[32,960]{1,0:T(8,128)}, u32[]{:S(2)}) copy-start(f32[32,960]{1,0:T(8,128)} %param.17) | copy-start | bytes 368644
  7.2 331.9 %all-reduce.5.cloned.1.call-start = ((), (), s32[]{:S(2)}) async-start(), calls=%async_computation | async-start | bytes 245760
  113.7 52.1 %copy-start.5 = (f32[8,64]{1,0:T(8,128)S(1)}, f32[8,64]{1,0:T(8,128)}, u32[]{:S(2)}) copy-start(f32[8,64]{1,0:T(8,128)} %param.24) | copy-start | bytes 6148
  113.7 52.1 %copy-start.6 = (s32[128,1]{0,1:T(1,128)S(1)}, s32[128,1]{0,1:T(1,128)}, u32[]{:S(2)}) copy-start(s32[128,1]{0,1:T(1,128)} %param.23) | copy-start | bytes 1540
  113.7 52.2 %copy-start.4 = (f32[8,128]{1,0:T(8,128)S(1)}, f32[8,128]{1,0:T(8,128)}, u32[]{:S(2)}) copy-start(f32[8,128]{1,0:T(8,128)} %param.25) | copy-start | bytes 12292
  120.2 3.1 copy-start.1
  214.7 0.7 copy-start.2
  222.1 11.1 %copy-start.3 = (f32[32,256]{1,0:T(8,128)S(1)}, f32[32,256]{1,0:T(8,128)}, u32[]{:S(2)}) copy-start(f32[32,256]{1,0:T(8,128)} %param.15) | copy-start | bytes 98308
Sparse Core Ops, SparseCore 0:
  215.5 123.5 all-reduce.4
